TPU v7x, 32 devices: a whole 2x2x4 slice. The times are simulated.
32 devices in a mesh: tm: 4 (over z), query: 2 (over y), rec: 4 (over x, core).
Axes of the slice: x: 2, y: 2, z: 4, core: 2. Of those that a mesh axis runs over, the one named last changes fastest.
Arguments:
- frames: bfloat16 [4, 2048, 1024], P('rec', 'tm'), may hold values from -100 to 100
- queries: bfloat16 [4096, 1024], P('query'), may hold values from -10 to 10
- kernel: float32 [33, 4096], P(None, 'query'), may hold values from 0.01 to 0.12
- labels: int32 [4, 2048], P('rec', 'tm'), may hold values from 0 to 4095
- lengths: int32 [4], P('rec'), may hold values from 512 to 2048, as said below
Outputs:
- grad_frames: bfloat16 [4, 2048, 1024], P('rec', 'tm', 'query')
- grad_queries: bfloat16 [4096, 1024], P('query', 'rec')
- grad_kernel: float32 [33, 4096], P(None, 'query')
Inputs may be any that keep to these rules, and one draw needn't show every extreme that they name: `lengths`: each entry counts the valid frames at the start of its recording; at least one recording has all 2048 frames valid.
All inputs are finite; a program needn't handle non-finite values.
Results may differ from a plain program's by a relative error of at most 0.0049.
Values sent between devices are 32-bit elements; how exact they have to be, the bound alone decides.
A program may use at most 64 MiB of HBM per device.

v0:
```python
import math
import jax
import jax.numpy as jnp
from jax import lax
from jax.sharding import PartitionSpec as P


def merged(x, axis, combine):
    peers = lax.axis_size(axis)
    step = 1
    while step < peers:
        swap = [(i, i ^ step) for i in range(peers)]
        x = combine(x, lax.ppermute(x, axis, swap))
        step *= 2
    return x


def halo_rows(x, axis, width):
    peers = lax.axis_size(axis)
    up = [(i, i + 1) for i in range(peers - 1)]
    down = [(i + 1, i) for i in range(peers - 1)]
    before = lax.ppermute(x[x.shape[0] - width :], axis, up)
    after = lax.ppermute(x[:width], axis, down)
    return lax.optimization_barrier((before, after))


def tap_sum(kernel, padded, row_count, flipped):
    tap_count = kernel.shape[0]
    running = jnp.zeros((row_count, padded.shape[1]), jnp.float32)
    for offset in range(tap_count):
        begin_row = tap_count - 1 - offset if flipped else offset
        running = running + kernel[offset][None, :] * padded[begin_row : begin_row + row_count]
    return running


def combine_stats(first_pair, second_pair):
    top_value = jnp.maximum(first_pair[0], second_pair[0])
    total_value = first_pair[1] * jnp.exp(first_pair[0] - top_value) + second_pair[1] * jnp.exp(
        second_pair[0] - top_value
    )
    return jnp.stack([top_value, total_value])


def row_softmax(smooth):
    local_top = jnp.max(smooth, axis=1)
    local_total = jnp.sum(jnp.exp(smooth - local_top[:, None]), axis=1)
    stats = merged(jnp.stack([local_top, local_total]), "query", combine_stats)
    top_value, total_value = (stats[0], stats[1])
    return jnp.exp(smooth - top_value[:, None]) / total_value[:, None]


def per_device(frames, queries, kernel, labels, lengths):
    frame_rows = frames[0]
    label_ids = labels[0]
    length_now = lengths[0]
    row_count = frame_rows.shape[0]
    query_count = queries.shape[0]
    width = frame_rows.shape[1]
    tap_count = kernel.shape[0]
    rim_width = tap_count // 2
    logit_scale = 10.0 / math.sqrt(width)
    frame_start = lax.axis_index("tm") * row_count
    is_valid = frame_start + jnp.arange(row_count, dtype=jnp.int32) < length_now
    query_start = lax.axis_index("query") * query_count
    query_ids = query_start + jnp.arange(query_count, dtype=jnp.int32)
    halo = 2 * rim_width
    tagged = jnp.concatenate(
        [
            frame_rows.astype(jnp.float32),
            jnp.broadcast_to(label_ids.astype(jnp.float32)[:, None], (row_count, 128)),
        ],
        axis=1,
    )
    before, after = halo_rows(tagged, "tm", halo)
    rim_rows = jnp.concatenate([before[:, :width], after[:, :width]]).astype(jnp.bfloat16)

    def scored(rows):
        return (
            lax.dot_general(
                rows, queries, (((1,), (1,)), ((), ())), preferred_element_type=jnp.float32
            )
            * logit_scale
        )

    inner = scored(frame_rows)
    rim = scored(rim_rows)
    wide = jnp.concatenate([rim[:halo], inner, rim[halo:]])
    wide_frames = frame_start - halo + jnp.arange(row_count + 2 * halo, dtype=jnp.int32)
    wide_valid = (wide_frames >= 0) & (wide_frames < length_now)
    wide = jnp.where(wide_valid[:, None], wide, 0.0)
    label_pad = jnp.concatenate(
        [
            before[halo - rim_width :, width].astype(jnp.int32),
            label_ids,
            after[:rim_width, width].astype(jnp.int32),
        ]
    )
    ext_rows = row_count + 2 * rim_width
    ext_frames = frame_start - rim_width + jnp.arange(ext_rows, dtype=jnp.int32)
    ext_valid = (ext_frames >= 0) & (ext_frames < length_now)
    smooth = tap_sum(kernel, wide, ext_rows, False)
    softmax_out = row_softmax(smooth)
    positive = (label_pad[:, None] == query_ids[None, :]).astype(jnp.float32)
    grad_pad = jnp.where(ext_valid[:, None], softmax_out - positive, 0.0)
    map_grad = grad_pad[rim_width : rim_width + row_count]
    padded = wide[rim_width : rim_width + row_count + 2 * rim_width]
    score_grad = tap_sum(kernel, grad_pad, row_count, True)
    score_grad = jnp.where(is_valid[:, None], score_grad, 0.0).astype(jnp.bfloat16)
    frame_part = jnp.dot(score_grad, queries, preferred_element_type=jnp.float32)
    frame_sum = lax.psum_scatter(frame_part, "query", scatter_dimension=1, tiled=True)
    grad_frames = (frame_sum * logit_scale).astype(jnp.bfloat16)[None]
    query_part = lax.dot_general(
        score_grad, frame_rows, (((0,), (0,)), ((), ())), preferred_element_type=jnp.float32
    )
    kernel_part = jnp.stack(
        [
            jnp.sum(map_grad * padded[offset : offset + row_count], axis=0)
            for offset in range(tap_count)
        ]
    )
    query_cols = lax.psum_scatter(query_part, "rec", scatter_dimension=1, tiled=True)
    query_cols, grad_kernel = lax.psum((query_cols, lax.psum(kernel_part, "rec")), "tm")
    grad_queries = (query_cols * logit_scale).astype(jnp.bfloat16)
    return (grad_frames, grad_queries, grad_kernel)


def solution(mesh):
    in_specs = (P("rec", "tm", None), P("query", None), P(None, "query"), P("rec", "tm"), P("rec"))
    out_specs = (P("rec", "tm", "query"), P("query", "rec"), P(None, "query"))
    return jax.shard_map(
        per_device, mesh=mesh, in_specs=in_specs, out_specs=out_specs, check_vma=False
    )
```

profile of v0, /device:TPU:0, one launch (start us, length us, event | category | flops | bytes accessed | tf_op | source)
XLA Modules:
  0.0 354.0 jit_solution(133784667908076871)
XLA Ops:
  7.2 0.0 copy-start.1
  7.2 0.0 all-reduce.4.cloned.1.call-start
  7.2 0.8 convert_element_type.36
  8.0 1.5 bitcast_convert_fusion
  9.5 0.1 broadcast_in_dim.54
  9.7 1.3 collective-permute-start.1
  11.0 5.6 %collective-permute-start = (f32[32,1152]{1,0:T(8,128)S(1)}, f32[32,1152]{1,0:T(8,128)S(1)}, u32[]{:S(2)}, u32[]{:S(2)}) collective-permute-start(f32[32,1152]{1,0:T(8,128)S(1)} %get-tuple-element.55), channel_id=1, source_target_pairs={{0,8},{8,16},{16,24},{1,9},{9,17},{17,25},{2,10},{10,18},{18,26},{... | collective-permute-start | bytes 442376 | tf_op jit(solution)/shard_map/ppermute | solution.py:22
  16.6 0.0 copy-done.2
  16.6 0.1 fusion.117
  16.7 0.1 fusion.116
  16.8 0.0 copy-start.3
  16.8 0.0 copy-start.5
  16.8 0.0 copy-start.7
  17.5 0.0 copy-done.1
  17.5 6.5 %convolution_multiply_fusion = f32[512,2048]{1,0:T(8,128)} fusion(bf16[2048,1024]{1,0:T(8,128)(2,1)} %param.6, bf16[1,512,1024]{2,1,0:T(8,128)(2,1)S(1)} %copy-done.1), kind=kOutput, calls=%fused_computation.200 | convolution fusion | flops 2148532224 | bytes 9437184 | tf_op jit(solution)/shard_map/dot_general | solution.py:79
  24.1 0.0 collective-permute-done.1
  24.1 0.0 collective-permute-done
  24.1 0.1 convert_reduce_fusion
  24.2 3.7 %convolution_multiply_fusion.1 = f32[64,2048]{1,0:T(8,128)S(1)} fusion(bf16[2048,1024]{1,0:T(8,128)(2,1)} %param.6, bf16[32,1024]{1,0:T(8,128)(2,1)S(1)} %slice.1206, bf16[32,1024]{1,0:T(8,128)(2,1)S(1)} %slice.1207), kind=kOutput, calls=%fused_computation.201 | convolution fusion | flops 268828672 | bytes 4849664 | tf_op jit(solution)/shard_map/dot_general | solution.py:79
  28.0 0.4 maximum_select_fusion
  28.5 22.3 %fusion.113 = (f32[544]{0:T(1024)S(1)}, f32[544,2048]{1,0:T(8,128)S(1)}) fusion(f32[576,2048]{1,0:T(8,128)S(1)} %maximum_select_fusion, f32[2048]{0:T(1024)S(1)} %bitcast.108, f32[2048]{0:T(1024)S(1)} %bitcast.110, f32[2048]{0:T(1024)S(1)} %bitcast.114, f32[2048]{0:T(1024)S(1)} %bitcast.116, f32[2048]{0:T(1024)S(1)} %bitcast.118, f32[2048]{0:T(1024)S(1)} %bitcast.120, ...), kind=kLoop, calls=%fused_computation.234 | loop fusion | flops 73530848 | bytes 151791744 | tf_op jit(solution)/shard_map/reduce_max | solution.py:45
  50.8 0.0 copy-start.17
  50.8 0.7 exponential_reduce_fusion
  51.6 2.0 collective-permute-start.2
  53.6 0.1 pad_add_fusion
  53.7 1.6 collective-permute-done.2
  55.3 1.5 subtract_select_fusion
  56.8 5.9 %fusion.49 = (f32[2048]{0:T(1024)}, f32[2048]{0:T(1024)}, f32[2048]{0:T(1024)}, f32[2048]{0:T(1024)}, f32[2048]{0:T(1024)}, /*index=5*/f32[2048]{0:T(1024)}, f32[2048]{0:T(1024)}, f32[2048]{0:T(1024)}, f32[2048]{0:T(1024)}) fusion(f32[576,2048]{1,0:T(8,128)S(1)} %maximum_select_fusion, f32[544,2048]{1,0:T(8,128)S(1)} %subtract_select_fusion), kind=kLoop, calls=%fused_computation.103 | loop fusion | flops 18855936 | bytes 42016768 | tf_op jit(solution)/shard_map/reduce_sum | solution.py:117
  62.7 5.6 %fusion.32 = (f32[2048]{0:T(1024)}, f32[2048]{0:T(1024)}, f32[2048]{0:T(1024)}, f32[2048]{0:T(1024)}, f32[2048]{0:T(1024)}, /*index=5*/f32[2048]{0:T(1024)}, f32[2048]{0:T(1024)}, f32[2048]{0:T(1024)}, f32[2048]{0:T(1024)}) fusion(f32[576,2048]{1,0:T(8,128)S(1)} %maximum_select_fusion, f32[544,2048]{1,0:T(8,128)S(1)} %subtract_select_fusion), kind=kLoop, calls=%fused_computation.69 | loop fusion | flops 18855936 | bytes 42016768 | tf_op jit(solution)/shard_map/reduce_sum | solution.py:117
  68.3 8.5 %fusion.40 = (f32[2048]{0:T(1024)}, f32[2048]{0:T(1024)}, f32[2048]{0:T(1024)}, f32[2048]{0:T(1024)}, f32[2048]{0:T(1024)}, /*index=5*/f32[2048]{0:T(1024)}, f32...) fusion(f32[576,2048]{1,0:T(8,128)S(1)} %maximum_select_fusion, ...), kind=kLoop, calls=%fused_computation.85 | loop fusion | flops 31426560 | bytes 67231744 | tf_op jit(solution)/shard_map/reduce_sum | solution.py:117
  76.9 17.9 %fusion.67 = bf16[512,2048]{1,0:T(8,128)(2,1)S(1)} fusion(f32[544,2048]{1,0:T(8,128)S(1)} %subtract_select_fusion, f32[2048]{0:T(1024)S(1)} %bitcast.109, f32[2048]{0:T(1024)S(1)} %bitcast.111, f32[2048]{0:T(1024)S(1)} %bitcast.115, f32[2048]{0:T(1024)S(1)} %bitcast.117, f32[2048]{0:T(1024)S(1)} %bitcast.119, f32[2048]{0:T(1024)S(1)} %bitcast.121, ...), kind=kLoop, calls=%fused_computation.137 | loop fusion | flops 70254592 | bytes 140780032 | tf_op jit(solution)/shard_map/convert_element_type | solution.py:108
  94.8 7.5 %stack.147 = f32[33,2048]{1,0:T(8,128)} concatenate(f32[1,2048]{1,0:T(1,128)} %bitcast.160, f32[1,2048]{1,0:T(1,128)} %bitcast.177, f32[1,2048]{1,0:T(1,128)} %bitcast.178, f32[1,2048]{1,0:T(1,128)} %bitcast.179, f32[1,2048]{1,0:T(1,128)} %bitcast.180, f32[1,2048]{1,0:T(1,128)} %bitcast.181, f32[1,2048]{1,0:T(1,128)} %bitcast.182, f32[1,2048]{1,0:T(1,128)} %bitcast.158, ...), dimensions={0} | concatenate | bytes 540672 | tf_op jit(solution)/shard_map/stack | solution.py:115
  102.2 0.0 all-reduce.4.cloned.1.call-update
  102.3 0.0 reduce-scatter.5.cloned.1.call-start
  102.3 6.8 %fusion.99 = f32[2048,1024]{1,0:T(8,128)} fusion(bf16[512,2048]{1,0:T(8,128)(2,1)S(1)} %fusion.67, bf16[1,512,1024]{2,1,0:T(8,128)(2,1)} %param.5), kind=kOutput, calls=%fused_computation.203 | convolution fusion | flops 2147483648 | bytes 11534336 | tf_op jit(solution)/shard_map/dot_general | solution.py:112
  109.2 0.0 reduce-scatter.5.cloned.1.call-update
  109.2 0.0 reduce-scatter.3.cloned.1.call-start
  109.2 5.8 %fusion.118 = f32[512,1024]{1,0:T(8,128)} fusion(bf16[512,2048]{1,0:T(8,128)(2,1)S(1)} %fusion.67, bf16[2048,1024]{1,0:T(8,128)(2,1)} %param.6), kind=kOutput, calls=%fused_computation.238 | convolution fusion | flops 2147483648 | bytes 8388608 | tf_op jit(solution)/shard_map/dot_general | solution.py:109
  115.1 0.0 reduce-scatter.3.cloned.1.call-update
  115.1 0.0 all-reduce.6.cloned.1.call-start
  115.2 20.5 %all-reduce.4.cloned.1.call-done = f32[33,2048]{1,0:T(8,128)} async-done(((f32[33,2048]{1,0:T(8,128)}), f32[33,2048]{1,0:T(8,128)}) %all-reduce.4.cloned.1.call-update) | async-done | bytes 270352 | tf_op jit(solution)/shard_map/psum | solution.py:122
  135.6 73.9 %reduce-scatter.5.cloned.1.call-done = f32[2048,256]{1,0:T(8,128)} async-done(((f32[2048,1024]{1,0:T(8,128)}), f32[2048,256]{1,0:T(8,128)}) %reduce-scatter.5.cloned.1.call-update) | async-done | bytes 2097168 | tf_op jit(solution)/shard_map/reduce_scatter | solution.py:121
  209.5 0.0 all-reduce.6.cloned.1.call-update
  209.5 34.2 %reduce-scatter.3.cloned.1.call-done = f32[512,512]{1,0:T(8,128)} async-done(((f32[512,1024]{1,0:T(8,128)}), f32[512,512]{1,0:T(8,128)}) %reduce-scatter.3.cloned.1.call-update) | async-done | bytes 1048592 | tf_op jit(solution)/shard_map/reduce_scatter | solution.py:110
  243.7 2.1 fusion.102
  245.8 97.2 %all-reduce.6.cloned.1.call-done = (f32[2048,256]{1,0:T(8,128)}, f32[33,2048]{1,0:T(8,128)}) async-done(((f32[2048,256]{1,0:T(8,128)}, f32[33,2048]{1,0:T(8,128)}), (f32[2048,256]{1,0:T(8,128)}, f32[33,2048]{1,0:T(8,128)})) %all-reduce.6.cloned.1.call-update) | async-done | bytes 2367504 | tf_op jit(solution)/shard_map/psum | solution.py:122
  343.0 2.7 multiply_convert_fusion
  345.8 1.7 copy.12
  (42 shorter events, 0.2 us)
Async XLA Ops:
  7.2 10.4 %copy-start.1 = (bf16[1,512,1024]{2,1,0:T(8,128)(2,1)S(1)}, bf16[1,512,1024]{2,1,0:T(8,128)(2,1)}, u32[]{:S(2)}) copy-start(bf16[1,512,1024]{2,1,0:T(8,128)(2,1)} %param.5) | copy-start | bytes 3145732
  7.2 9.4 %copy-start.2 = (f32[33,2048]{1,0:T(8,128)S(1)}, f32[33,2048]{1,0:T(8,128)}, u32[]{:S(2)}) copy-start(f32[33,2048]{1,0:T(8,128)} %param.7) | copy-start | bytes 811012
  7.2 128.4 %all-reduce.4.cloned.1.call-start = ((), (), s32[]{:S(2)}) async-start(), calls=%async_computation.4 | async-start | bytes 655360 | tf_op jit(solution)/shard_map/psum | solution.py:122
  9.7 14.4 %collective-permute-start.1 = (f32[32,1152]{1,0:T(8,128)S(1)}, f32[32,1152]{1,0:T(8,128)S(1)}, u32[]{:S(2)}, u32[]{:S(2)}) collective-permute-start(f32[32,1152]{1,0:T(8,128)S(1)} %get-tuple-element.54), channel_id=1, source_target_pairs={{8,0},{16,8},{24,16},{9,1},{17,9},{25,17},{10,2},{18,10},{26,18},{... | collective-permute-start | bytes 442376 | tf_op jit(solution)/shard_map/ppermute | solution.py:23
  11.0 13.1 %collective-permute-start = (f32[32,1152]{1,0:T(8,128)S(1)}, f32[32,1152]{1,0:T(8,128)S(1)}, u32[]{:S(2)}, u32[]{:S(2)}) collective-permute-start(f32[32,1152]{1,0:T(8,128)S(1)} %get-tuple-element.55), channel_id=1, source_target_pairs={{0,8},{8,16},{16,24},{1,9},{9,17},{17,25},{2,10},{10,18},{18,26},{... | collective-permute-start | bytes 442376 | tf_op jit(solution)/shard_map/ppermute | solution.py:22
  16.8 11.6 %copy-start.3 = (f32[1,2048]{1,0:T(1,128)}, f32[1,2048]{1,0:T(1,128)S(1)}, u32[]{:S(2)}) copy-start(f32[1,2048]{1,0:T(1,128)S(1)} %get-tuple-element.70) | copy-start | bytes 24580
  16.8 11.6 %copy-start.5 = (f32[1,2048]{1,0:T(1,128)}, f32[1,2048]{1,0:T(1,128)S(1)}, u32[]{:S(2)}) copy-start(f32[1,2048]{1,0:T(1,128)S(1)} %get-tuple-element.71) | copy-start | bytes 24580
  16.8 11.6 %copy-start.7 = (f32[1,2048]{1,0:T(1,128)}, f32[1,2048]{1,0:T(1,128)S(1)}, u32[]{:S(2)}) copy-start(f32[1,2048]{1,0:T(1,128)S(1)} %get-tuple-element.72) | copy-start | bytes 24580
  16.8 11.6 %copy-start.9 = (f32[1,2048]{1,0:T(1,128)}, f32[1,2048]{1,0:T(1,128)S(1)}, u32[]{:S(2)}) copy-start(f32[1,2048]{1,0:T(1,128)S(1)} %get-tuple-element.73) | copy-start | bytes 24580
  16.8 11.6 %copy-start.11 = (f32[1,2048]{1,0:T(1,128)}, f32[1,2048]{1,0:T(1,128)S(1)}, u32[]{:S(2)}) copy-start(f32[1,2048]{1,0:T(1,128)S(1)} %get-tuple-element.74) | copy-start | bytes 24580
  16.9 11.6 %copy-start.13 = (f32[1,2048]{1,0:T(1,128)}, f32[1,2048]{1,0:T(1,128)S(1)}, u32[]{:S(2)}) copy-start(f32[1,2048]{1,0:T(1,128)S(1)} %get-tuple-element.75) | copy-start | bytes 24580
  16.9 11.6 %copy-start.15 = (f32[1,2048]{1,0:T(1,128)}, f32[1,2048]{1,0:T(1,128)S(1)}, u32[]{:S(2)}) copy-start(f32[1,2048]{1,0:T(1,128)S(1)} %get-tuple-element.76) | copy-start | bytes 24580
  24.1 4.0 %copy-start = (f32[512,2048]{1,0:T(8,128)S(1)}, f32[512,2048]{1,0:T(8,128)}, u32[]{:S(2)}) copy-start(f32[512,2048]{1,0:T(8,128)} %convolution_multiply_fusion) | copy-start | bytes 12582916
  50.8 2.8 copy-start.17
  51.6 3.7 %collective-permute-start.2 = (f32[2,544]{1,0:T(2,128)S(1)}, f32[2,544]{1,0:T(2,128)S(1)}, u32[]{:S(2)}, u32[]{:S(2)}) collective-permute-start(f32[2,544]{1,0:T(2,128)S(1)} %pad_maximum_fusion.2), channel_id=1, source_target_pairs={{0,4},{4,0},{1,5},{5,1},{2,6},{6,2},{3,7},{7,3},{8,12},{12,8},{9,1... | collective-permute-start | bytes 13064 | tf_op jit(solution)/shard_map/ppermute | solution.py:13
  68.3 8.6 %copy-start.4 = (f32[1,2048]{1,0:T(1,128)S(1)}, f32[1,2048]{1,0:T(1,128)}, u32[]{:S(2)}) copy-start(f32[1,2048]{1,0:T(1,128)} %copy-done.3) | copy-start | bytes 24580
  68.3 8.6 %copy-start.6 = (f32[1,2048]{1,0:T(1,128)S(1)}, f32[1,2048]{1,0:T(1,128)}, u32[]{:S(2)}) copy-start(f32[1,2048]{1,0:T(1,128)} %copy-done.5) | copy-start | bytes 24580
  68.3 8.6 %copy-start.8 = (f32[1,2048]{1,0:T(1,128)S(1)}, f32[1,2048]{1,0:T(1,128)}, u32[]{:S(2)}) copy-start(f32[1,2048]{1,0:T(1,128)} %copy-done.7) | copy-start | bytes 24580
  68.3 8.6 %copy-start.10 = (f32[1,2048]{1,0:T(1,128)S(1)}, f32[1,2048]{1,0:T(1,128)}, u32[]{:S(2)}) copy-start(f32[1,2048]{1,0:T(1,128)} %copy-done.9) | copy-start | bytes 24580
  68.3 8.6 %copy-start.12 = (f32[1,2048]{1,0:T(1,128)S(1)}, f32[1,2048]{1,0:T(1,128)}, u32[]{:S(2)}) copy-start(f32[1,2048]{1,0:T(1,128)} %copy-done.11) | copy-start | bytes 24580
  68.3 8.6 %copy-start.14 = (f32[1,2048]{1,0:T(1,128)S(1)}, f32[1,2048]{1,0:T(1,128)}, u32[]{:S(2)}) copy-start(f32[1,2048]{1,0:T(1,128)} %copy-done.13) | copy-start | bytes 24580
  68.3 8.6 %copy-start.16 = (f32[1,2048]{1,0:T(1,128)S(1)}, f32[1,2048]{1,0:T(1,128)}, u32[]{:S(2)}) copy-start(f32[1,2048]{1,0:T(1,128)} %copy-done.15) | copy-start | bytes 24580
  102.3 107.2 %reduce-scatter.5.cloned.1.call-start = ((), (), s32[]{:S(2)}) async-start(), calls=%async_computation.3 | async-start | bytes 10485760 | tf_op jit(solution)/shard_map/reduce_scatter | solution.py:121
  109.2 134.5 %reduce-scatter.3.cloned.1.call-start = ((), (), s32[]{:S(2)}) async-start(), calls=%async_computation.2 | async-start | bytes 3145728 | tf_op jit(solution)/shard_map/reduce_scatter | solution.py:110
  115.1 227.9 %all-reduce.6.cloned.1.call-start = ((), (), s32[]{:S(2)}) async-start(), calls=%async_computation.5 | async-start | bytes 4849664 | tf_op jit(solution)/shard_map/psum | solution.py:122
Sparse Core Ops, SparseCore 0:
  102.4 33.2 all-reduce.3
  138.2 71.2 reduce-scatter.4
  211.8 31.8 reduce-scatter.2
  246.0 97.0 all-reduce.5
where the time goes:
time: 355 us; the launch traced here: 354 us
  waiting for transfers between devices  227 us (64%)
  other arithmetic  70.2 us (20%)
  matrix products  22.9 us (6%)
  between operations  14.8 us (4%)
  local copies, waits for them, and re-layouts  9.67 us (3%)
  starting transfers between devices  9.07 us (3%)
    psum x1, waiting for transfers between devices, per_device(): lax.psum((query_cols, lax.psum(kernel_part, 'rec')), 'tm')  97.2 us
    reduce_scatter x1, waiting for transfers between devices, per_device(): lax.psum_scatter(query_part, 'rec', scatter_dimension=1, tiled=True)  73.9 us
    reduce_scatter x1, waiting for transfers between devices, per_device(): lax.psum_scatter(frame_part, 'query', scatter_dimension=1, tiled=True)  34.2 us
    reduce_max x1, other arithmetic, row_softmax(): local_top = jnp.max(smooth, axis=1)  22.3 us
    psum x1, waiting for transfers between devices, per_device(): lax.psum(kernel_part, 'rec')  20.5 us
    reduce_sum x3, other arithmetic, per_device(): jnp.sum(map_grad * padded[offset:offset + row_count], axis=0)  20 us
    convert_element_type x1, other arithmetic, per_device(): jnp.where(is_valid[:, None], score_grad, 0.0).astype(jnp.bfloat16)  17.9 us
    dot_general x2, matrix products, scored(): lax.dot_general(rows, queries, (((1,), (1,)), ((), ())), preferred_elemen...  10.2 us
  transfers between devices with their start and end apart: 7, of which 5 were waited for; matrix products, arithmetic and copies ran while one was open for 6% of the time, Pallas kernels for 0%

commit v1 on v0

--- a/solution.py
+++ b/solution.py
@@ -119,7 +119,9 @@
         ]
     )
     query_cols = lax.psum_scatter(query_part, "rec", scatter_dimension=1, tiled=True)
-    query_cols, grad_kernel = lax.psum((query_cols, lax.psum(kernel_part, "rec")), "tm")
+    query_cols, grad_kernel = lax.psum(
+        (query_cols, jnp.sum(lax.all_gather(kernel_part, "rec"), axis=0)), "tm"
+    )
     grad_queries = (query_cols * logit_scale).astype(jnp.bfloat16)
     return (grad_frames, grad_queries, grad_kernel)
 

time: 355 us -> 371 us (1.045)
  other arithmetic: 70.2 us -> 122 us
  waiting for transfers between devices: 227 us -> 197 us
  local copies, waits for them, and re-layouts: 9.67 us -> 5.69 us
    convert_element_type x1, other arithmetic: 17.9 us -> 69.7 us  [per_device(): jnp.where(is_valid[:, None], score_grad, 0.0).astype(jnp.bfloat16)]
    psum x2 -> x1, waiting for transfers between devices: 118 us -> 97.8 us  [per_device(): lax.psum((query_cols, jnp.sum(lax.all_gather(kernel_part, 'rec'), axis=0)...]
    reduce_scatter x1, waiting for transfers between devices: 73.9 us -> 63.9 us  [per_device(): lax.psum_scatter(query_part, 'rec', scatter_dimension=1, tiled=True)]
    another operation x1, local copies, waits for them, and re-layouts: 7.47 us -> 3.54 us  [per_device(): jnp.stack([jnp.sum(map_grad * padded[offset:offset + row_count], axis=0)...]
  transfers between devices with their start and end apart: 7 -> 7, of which waited for: 5 -> 4; matrix products, arithmetic and copies ran while one was open for 6% -> 25% of each run, Pallas kernels for 0% -> 0%
where the time goes in v1:
time: 371 us
  waiting for transfers between devices  197 us (53%)
  other arithmetic  122 us (33%)
  matrix products  21.7 us (6%)
  between operations  14.7 us (4%)
  starting transfers between devices  9.07 us (2%)
  local copies, waits for them, and re-layouts  5.69 us (2%)
    psum x1, waiting for transfers between devices, per_device(): lax.psum((query_cols, jnp.sum(lax.all_gather(kernel_part, 'rec'), axis=0)...  97.8 us
    convert_element_type x1, other arithmetic, per_device(): jnp.where(is_valid[:, None], score_grad, 0.0).astype(jnp.bfloat16)  69.7 us
    reduce_scatter x1, waiting for transfers between devices, per_device(): lax.psum_scatter(query_part, 'rec', scatter_dimension=1, tiled=True)  63.9 us
    reduce_scatter x1, waiting for transfers between devices, per_device(): lax.psum_scatter(frame_part, 'query', scatter_dimension=1, tiled=True)  34.2 us
    reduce_max x1, other arithmetic, row_softmax(): local_top = jnp.max(smooth, axis=1)  22.2 us
    reduce_sum x3, other arithmetic, per_device(): jnp.sum(map_grad * padded[offset:offset + row_count], axis=0)  18.1 us
    dot_general x2, matrix products, scored(): lax.dot_general(rows, queries, (((1,), (1,)), ((), ())), preferred_elemen...  10.2 us
  transfers between devices with their start and end apart: 7, of which 4 were waited for; matrix products, arithmetic and copies ran while one was open for 25% of the time, Pallas kernels for 0%

profile of v1, /device:TPU:0, one launch (start us, length us, event | category | flops | bytes accessed | tf_op | source)
XLA Modules:
  0.0 370.9 jit_solution(6828058956509358287)
XLA Ops:
  7.2 0.0 copy-start.2
  7.2 0.0 all-gather.4.cloned.1.call-start
  7.2 0.8 convert_element_type.36
  8.0 1.5 bitcast_convert_fusion
  9.5 0.1 broadcast_in_dim.54
  9.7 1.3 collective-permute-start.1
  11.0 5.6 %collective-permute-start = (f32[32,1152]{1,0:T(8,128)S(1)}, f32[32,1152]{1,0:T(8,128)S(1)}, u32[]{:S(2)}, u32[]{:S(2)}) collective-permute-start(f32[32,1152]{1,0:T(8,128)S(1)} %get-tuple-element.55), channel_id=1, source_target_pairs={{0,8},{8,16},{16,24},{1,9},{9,17},{17,25},{2,10},{10,18},{18,26},{... | collective-permute-start | bytes 442376 | tf_op jit(solution)/shard_map/ppermute | solution.py:22
  16.6 0.0 copy-done.3
  16.6 0.1 fusion.117
  16.7 0.1 fusion.116
  17.5 6.5 %convolution_multiply_fusion = f32[512,2048]{1,0:T(8,128)} fusion(bf16[2048,1024]{1,0:T(8,128)(2,1)} %param.6, bf16[1,512,1024]{2,1,0:T(8,128)(2,1)S(1)} %copy-done.2), kind=kOutput, calls=%fused_computation.200 | convolution fusion | flops 2148532224 | bytes 9437184 | tf_op jit(solution)/shard_map/dot_general | solution.py:79
  24.0 0.0 copy-start.1
  24.0 0.0 collective-permute-done.1
  24.0 0.0 collective-permute-done
  24.0 0.1 convert_reduce_fusion
  24.2 3.7 %convolution_multiply_fusion.1 = f32[64,2048]{1,0:T(8,128)S(1)} fusion(bf16[2048,1024]{1,0:T(8,128)(2,1)} %param.6, bf16[32,1024]{1,0:T(8,128)(2,1)S(1)} %slice.1206, bf16[32,1024]{1,0:T(8,128)(2,1)S(1)} %slice.1207), kind=kOutput, calls=%fused_computation.201 | convolution fusion | flops 268828672 | bytes 4849664 | tf_op jit(solution)/shard_map/dot_general | solution.py:79
  28.0 0.4 maximum_select_fusion
  28.3 22.2 %fusion.113 = (f32[544]{0:T(1024)S(1)}, f32[544,2048]{1,0:T(8,128)S(1)}) fusion(f32[576,2048]{1,0:T(8,128)S(1)} %maximum_select_fusion, f32[2048]{0:T(1024)S(1)} %bitcast.110, f32[2048]{0:T(1024)S(1)} %bitcast.112, f32[2048]{0:T(1024)S(1)} %bitcast.116, f32[2048]{0:T(1024)S(1)} %bitcast.118, f32[2048]{0:T(1024)S(1)} %bitcast.120, f32[2048]{0:T(1024)S(1)} %bitcast.122, ...), kind=kLoop, calls=%fused_computation.234 | loop fusion | flops 73530848 | bytes 151791744 | tf_op jit(solution)/shard_map/reduce_max | solution.py:45
  50.6 0.0 copy-start.4
  50.6 0.7 exponential_reduce_fusion
  51.4 2.0 collective-permute-start.2
  53.4 0.0 copy-done.4
  53.4 0.1 pad_add_fusion
  53.5 1.6 collective-permute-done.2
  55.1 1.5 subtract_select_fusion
  56.6 0.0 copy-start
  56.6 5.3 %fusion.49 = (f32[2048]{0:T(1024)S(1)}, f32[2048]{0:T(1024)S(1)}, f32[2048]{0:T(1024)S(1)}, f32[2048]{0:T(1024)S(1)}, f32[2048]{0:T(1024)S(1)}, /*index=5*/f32[2...) fusion(f32[576,2048]{1,0:T(8,128)S(1)} %maximum_select_fusion, f32[544,2048]{1,0:T(8,128)S(1)} %subtract_select_fusion), kind=kLoop, calls=%fused_computation.103 | loop fusion | flops 18855936 | bytes 42016768 | tf_op jit(solution)/shard_map/reduce_sum | solution.py:117
  61.9 5.0 %fusion.32 = (f32[2048]{0:T(1024)S(1)}, f32[2048]{0:T(1024)S(1)}, f32[2048]{0:T(1024)S(1)}, f32[2048]{0:T(1024)S(1)}, f32[2048]{0:T(1024)S(1)}, /*index=5*/f32[2...) fusion(f32[576,2048]{1,0:T(8,128)S(1)} %maximum_select_fusion, f32[544,2048]{1,0:T(8,128)S(1)} %subtract_select_fusion), kind=kLoop, calls=%fused_computation.69 | loop fusion | flops 18855936 | bytes 42016768 | tf_op jit(solution)/shard_map/reduce_sum | solution.py:117
  66.9 7.8 %fusion.40 = (f32[2048]{0:T(1024)S(1)}, f32[2048]{0:T(1024)S(1)}, f32[2048]{0:T(1024)S(1)}, f32[2048]{0:T(1024)S(1)}, f32[2048]{0:T(1024)S(1)}, /*index=5*/f32[2...) fusion(f32[576,2048]{1,0:T(8,128)S(1)} %maximum_select_fusion, ...), kind=kLoop, calls=%fused_computation.85 | loop fusion | flops 31426560 | bytes 67231744 | tf_op jit(solution)/shard_map/reduce_sum | solution.py:117
  74.7 3.5 stack.147
  78.3 0.0 all-gather.4.cloned.1.call-update
  78.3 0.0 reduce-scatter.5.cloned.1.call-start
  78.4 69.7 %fusion.67 = bf16[512,2048]{1,0:T(8,128)(2,1)S(1)} fusion(f32[544,2048]{1,0:T(8,128)} %copy-done, f32[2048]{0:T(1024)S(1)} %bitcast.111, f32[2048]{0:T(1024)S(1)} %bitcast.113, f32[2048]{0:T(1024)S(1)} %bitcast.117, f32[2048]{0:T(1024)S(1)} %bitcast.119, f32[2048]{0:T(1024)S(1)} %bitcast.121, f32[2048]{0:T(1024)S(1)} %bitcast.123, f32[2048]{0:T(1024)S(1)} %bitcast.125, ...), kind=kLoop, calls=%fused_computation.137 | loop fusion | flops 70254592 | bytes 140780032 | tf_op jit(solution)/shard_map/convert_element_type | solution.py:108
  148.1 5.6 %fusion.99 = f32[2048,1024]{1,0:T(8,128)} fusion(bf16[512,2048]{1,0:T(8,128)(2,1)S(1)} %fusion.67, bf16[1,512,1024]{2,1,0:T(8,128)(2,1)S(1)} %copy-done.2), kind=kOutput, calls=%fused_computation.203 | convolution fusion | flops 2147483648 | bytes 11534336 | tf_op jit(solution)/shard_map/dot_general | solution.py:112
  153.7 0.0 reduce-scatter.5.cloned.1.call-update
  153.7 0.0 reduce-scatter.3.cloned.1.call-start
  153.8 5.8 %fusion.118 = f32[512,1024]{1,0:T(8,128)} fusion(bf16[512,2048]{1,0:T(8,128)(2,1)S(1)} %fusion.67, bf16[2048,1024]{1,0:T(8,128)(2,1)} %param.6), kind=kOutput, calls=%fused_computation.238 | convolution fusion | flops 2147483648 | bytes 8388608 | tf_op jit(solution)/shard_map/dot_general | solution.py:109
  159.6 0.0 reduce-scatter.3.cloned.1.call-update
  159.6 0.0 all-reduce.3.cloned.1.call-start
  159.7 0.0 all-gather.4.cloned.1.call-done
  159.7 2.2 reduce_sum.349
  161.9 63.9 %reduce-scatter.5.cloned.1.call-done = f32[2048,256]{1,0:T(8,128)} async-done(((f32[2048,1024]{1,0:T(8,128)}), f32[2048,256]{1,0:T(8,128)}) %reduce-scatter.5.cloned.1.call-update) | async-done | bytes 2097168 | tf_op jit(solution)/shard_map/reduce_scatter | solution.py:121
  225.8 0.0 all-reduce.3.cloned.1.call-update
  225.8 34.2 %reduce-scatter.3.cloned.1.call-done = f32[512,512]{1,0:T(8,128)} async-done(((f32[512,1024]{1,0:T(8,128)}), f32[512,512]{1,0:T(8,128)}) %reduce-scatter.3.cloned.1.call-update) | async-done | bytes 1048592 | tf_op jit(solution)/shard_map/reduce_scatter | solution.py:110
  260.0 2.1 fusion.102
  262.1 97.8 %all-reduce.3.cloned.1.call-done = (f32[2048,256]{1,0:T(8,128)}, f32[33,2048]{1,0:T(8,128)}) async-done(((f32[2048,256]{1,0:T(8,128)}, f32[33,2048]{1,0:T(8,128)}), (f32[2048,256]{1,0:T(8,128)}, f32[33,2048]{1,0:T(8,128)})) %all-reduce.3.cloned.1.call-update) | async-done | bytes 2367504 | tf_op jit(solution)/shard_map/psum | solution.py:122
  359.9 2.7 multiply_convert_fusion
  362.6 1.7 copy.11
  (17 shorter events, 0.2 us)
Async XLA Ops:
  7.2 10.3 %copy-start.2 = (bf16[1,512,1024]{2,1,0:T(8,128)(2,1)S(1)}, bf16[1,512,1024]{2,1,0:T(8,128)(2,1)}, u32[]{:S(2)}) copy-start(bf16[1,512,1024]{2,1,0:T(8,128)(2,1)} %param.5) | copy-start | bytes 3145732
  7.2 9.4 %copy-start.3 = (f32[33,2048]{1,0:T(8,128)S(1)}, f32[33,2048]{1,0:T(8,128)}, u32[]{:S(2)}) copy-start(f32[33,2048]{1,0:T(8,128)} %param.7) | copy-start | bytes 811012
  7.2 152.5 %all-gather.4.cloned.1.call-start = ((), (), s32[]{:S(2)}) async-start(), calls=%async_computation.4 | async-start | bytes 1638400 | tf_op jit(solution)/shard_map/all_gather | solution.py:123
  9.7 14.3 %collective-permute-start.1 = (f32[32,1152]{1,0:T(8,128)S(1)}, f32[32,1152]{1,0:T(8,128)S(1)}, u32[]{:S(2)}, u32[]{:S(2)}) collective-permute-start(f32[32,1152]{1,0:T(8,128)S(1)} %get-tuple-element.54), channel_id=1, source_target_pairs={{8,0},{16,8},{24,16},{9,1},{17,9},{25,17},{10,2},{18,10},{26,18},{... | collective-permute-start | bytes 442376 | tf_op jit(solution)/shard_map/ppermute | solution.py:23
  11.0 13.0 %collective-permute-start = (f32[32,1152]{1,0:T(8,128)S(1)}, f32[32,1152]{1,0:T(8,128)S(1)}, u32[]{:S(2)}, u32[]{:S(2)}) collective-permute-start(f32[32,1152]{1,0:T(8,128)S(1)} %get-tuple-element.55), channel_id=1, source_target_pairs={{0,8},{8,16},{16,24},{1,9},{9,17},{17,25},{2,10},{10,18},{18,26},{... | collective-permute-start | bytes 442376 | tf_op jit(solution)/shard_map/ppermute | solution.py:22
  24.0 4.0 %copy-start.1 = (f32[512,2048]{1,0:T(8,128)S(1)}, f32[512,2048]{1,0:T(8,128)}, u32[]{:S(2)}) copy-start(f32[512,2048]{1,0:T(8,128)} %convolution_multiply_fusion) | copy-start | bytes 12582916
  50.6 2.8 copy-start.4
  51.4 3.7 collective-permute-start.2
  56.6 10.3 %copy-start = (f32[544,2048]{1,0:T(8,128)}, f32[544,2048]{1,0:T(8,128)S(1)}, u32[]{:S(2)}) copy-start(f32[544,2048]{1,0:T(8,128)S(1)} %subtract_select_fusion) | copy-start | bytes 13369348
  78.3 147.5 %reduce-scatter.5.cloned.1.call-start = ((), (), s32[]{:S(2)}) async-start(), calls=%async_computation.3 | async-start | bytes 10485760 | tf_op jit(solution)/shard_map/reduce_scatter | solution.py:121
  153.7 106.2 %reduce-scatter.3.cloned.1.call-start = ((), (), s32[]{:S(2)}) async-start(), calls=%async_computation.2 | async-start | bytes 3145728 | tf_op jit(solution)/shard_map/reduce_scatter | solution.py:110
  159.6 200.3 %all-reduce.3.cloned.1.call-start = ((), (), s32[]{:S(2)}) async-start(), calls=%async_computation.5 | async-start | bytes 4849664 | tf_op jit(solution)/shard_map/psum | solution.py:122
Sparse Core Ops, SparseCore 0:
  78.4 18.8 all-gather.3
  153.9 71.8 reduce-scatter.4
  228.0 31.8 reduce-scatter.2
  262.8 96.9 all-reduce.2
